TPU v7x, 32 devices: a whole 2x2x4 slice. The times are simulated.
32 devices in a mesh: pb: 4 (over x, core), ka: 4 (over z), ga: 2 (over y).
Axes of the slice: x: 2, y: 2, z: 4, core: 2. Of those that a mesh axis runs over, the one named last changes fastest.
Arguments:
- queries: bfloat16 [16, 512, 768], P(None, 'pb', 'ga'), may hold values from -6 to 6
- comp_keys: bfloat16 [1024, 768], P(('ka', 'pb'), 'ga'), may hold values from -6 to 6
- comp_values: bfloat16 [1024, 512], P(('ka', 'pb'), 'ga'), may hold values from -6 to 6
- outputs: bfloat16 [16, 512, 512], P(None, 'pb', 'ga'), may hold values from -1.1953125 to 1.1953125
- grad_out: bfloat16 [16, 512, 512], P(None, 'pb', 'ga'), may hold values from -300 to 300
- log_sums: float32 [4, 16, 512], P('ga', None, 'pb'), may hold values from 7 to 10
- visible: int32 [8, 1024], P('pb', 'ka'), may hold values from 0 to 1, as said below
Outputs:
- grad_queries: float32 [16, 512, 768], P('ka', 'pb', 'ga')
- grad_keys: float32 [1024, 768], P(('ka', 'pb'), 'ga')
- grad_values: float32 [1024, 512], P(('ka', 'pb'), 'ga')
Inputs may be any that keep to these rules, and one draw needn't show every extreme that they name: The queries are the last 512 positions of a sequence of 16384 positions, and compressed key j covers positions 16 * j to 16 * j + 31. visible[b, j] is 1 exactly when key j ends before the first position of query block b and starts no earlier than the start of the document that holds that position; the sequence is packed from a few documents.
All inputs are finite; a program needn't handle non-finite values.
Results may differ from a plain program's by a relative error of at most 0.0029.
Values may be sent and summed in bfloat16 or wider, within the bound.
A program may use at most 64 MiB of HBM per device.

v0:
```python
import jax
import jax.numpy as jnp
from jax import lax
from jax.sharding import PartitionSpec as P

DK = 192
DV = 128
QBLK = 64


def group_grads(query_group, grad_group, row_delta, row_lse, key_group, value_group, mask_part):
    head_count, query_count, _ = query_group.shape
    length = key_group.shape[0]
    softmax_scale = DK ** (-0.5)
    scores = (
        jnp.einsum("hqd,kd->hqk", query_group, key_group, preferred_element_type=jnp.float32)
        * softmax_scale
    )
    weights = mask_part.astype(jnp.float32)[None, :, None, :]
    probs_full = (
        jnp.exp(scores - row_lse[:, :, None]).reshape(head_count, query_count // QBLK, QBLK, length)
        * weights
    )
    probs_full = probs_full.reshape(head_count, query_count, length)
    probs_low = probs_full.astype(jnp.bfloat16)
    grad_probs = jnp.einsum(
        "hqd,kd->hqk", grad_group, value_group, preferred_element_type=jnp.float32
    )
    grad_scores = (probs_full * (grad_probs - row_delta[:, :, None])).astype(jnp.bfloat16)
    value_grad = jnp.einsum(
        "hqk,hqd->kd", probs_low, grad_group, preferred_element_type=jnp.float32
    )
    key_grad = (
        jnp.einsum("hqk,hqd->kd", grad_scores, query_group, preferred_element_type=jnp.float32)
        * softmax_scale
    )
    query_grad = (
        jnp.einsum("hqk,kd->hqd", grad_scores, key_group, preferred_element_type=jnp.float32)
        * softmax_scale
    )
    return (query_grad, key_grad, value_grad)


def piece_grads(arrays, key_part, value_part, mask_part):
    queries, grad_out, deltas, log_sums = arrays
    groups = key_part.shape[1] // DK
    results = []
    for group_index in range(groups):
        results.append(
            group_grads(
                queries[:, :, group_index * DK : (group_index + 1) * DK],
                grad_out[:, :, group_index * DV : (group_index + 1) * DV],
                deltas[group_index],
                log_sums[group_index],
                key_part[:, group_index * DK : (group_index + 1) * DK],
                value_part[:, group_index * DV : (group_index + 1) * DV],
                mask_part,
            )
        )
    return (
        jnp.concatenate([entry[0] for entry in results], axis=2),
        jnp.concatenate([entry[1] for entry in results], axis=1),
        jnp.concatenate([entry[2] for entry in results], axis=1),
    )


def guarded(arrays, key_part, value_part, mask_part):
    return piece_grads(arrays, key_part, value_part, mask_part)


def key_blocks(arrays, key_part, value_part, mask_part):
    length = key_part.shape[0]
    block_rows = 512 if length > 512 and length % 512 == 0 else length
    number = length // block_rows
    if number == 1:
        return guarded(arrays, key_part, value_part, mask_part)
    key_stack = key_part.reshape(number, block_rows, key_part.shape[1])
    value_stack = value_part.reshape(number, block_rows, value_part.shape[1])
    mask_stack = mask_part.reshape(mask_part.shape[0], number, block_rows).transpose(1, 0, 2)

    def advance(running, inputs):
        query_grad, key_grad, value_grad = guarded(arrays, inputs[0], inputs[1], inputs[2])
        return (running + query_grad, (key_grad, value_grad))

    initial = jnp.zeros((arrays[0].shape[0], arrays[0].shape[1], key_part.shape[1]), jnp.float32)
    summed, (key_grads, value_grads) = lax.scan(
        advance, initial, (key_stack, value_stack, mask_stack)
    )
    return (
        summed,
        key_grads.reshape(length, key_part.shape[1]),
        value_grads.reshape(length, value_part.shape[1]),
    )


def per_device(queries, comp_keys, comp_values, outputs, grad_out, log_sums, visible):
    groups = comp_keys.shape[1] // DK
    deltas = jnp.stack(
        [
            jnp.einsum(
                "hqd,hqd->hq",
                grad_out[:, :, group_index * DV : (group_index + 1) * DV],
                outputs[:, :, group_index * DV : (group_index + 1) * DV],
                preferred_element_type=jnp.float32,
            )
            for group_index in range(groups)
        ]
    )
    arrays = (queries, grad_out, deltas, log_sums)
    whole_keys, whole_values = (
        lax.all_gather(comp_keys, "pb", axis=0, tiled=True),
        lax.all_gather(comp_values, "pb", axis=0, tiled=True),
    )
    unused, key_grad, value_grad = key_blocks(arrays, whole_keys, whole_values, visible)
    stacked = lax.psum_scatter(
        jnp.concatenate([key_grad, value_grad], axis=1), "pb", scatter_dimension=0, tiled=True
    )
    key_out = stacked[:, : groups * DK]
    value_out = stacked[:, groups * DK :]
    head_part = (queries, grad_out, deltas, log_sums)
    query_grad, unused_key, unused_value = key_blocks(head_part, whole_keys, whole_values, visible)
    query_out = lax.psum_scatter(query_grad, "ka", scatter_dimension=0, tiled=True)
    return (query_out, key_out, value_out)


def solution(mesh):
    return jax.shard_map(
        per_device,
        mesh=mesh,
        in_specs=(
            P(None, "pb", "ga"),
            P(("ka", "pb"), "ga"),
            P(("ka", "pb"), "ga"),
            P(None, "pb", "ga"),
            P(None, "pb", "ga"),
            P("ga", None, "pb"),
            P("pb", "ka"),
        ),
        out_specs=(P("ka", "pb", "ga"), P(("ka", "pb"), "ga"), P(("ka", "pb"), "ga")),
        check_vma=False,
    )
```

profile of v0, /device:TPU:0, one launch (start us, length us, event | category | flops | bytes accessed | tf_op | source)
XLA Modules:
  0.0 126.5 jit_solution(304562002769784514)
XLA Ops:
  7.2 0.8 convert_element_type.20
  8.0 0.7 slice_bitcast_fusion.11
  8.7 6.7 %all_gather.7 = bf16[256,256]{1,0:T(8,128)(2,1)S(1)} all-gather(bf16[64,256]{1,0:T(8,128)(2,1)} %param.9), channel_id=1, replica_groups=mesh['pb'=4,'ka'=4,'ga'=2] {'pb'}, dimensions={0}, use_global_device_ids=true | all-gather | bytes 163840 | tf_op jit(solution)/shard_map/all_gather | solution.py:112
  15.4 6.0 %all_gather.6 = bf16[256,384]{1,0:T(8,128)(2,1)S(1)} all-gather(bf16[64,384]{1,0:T(8,128)(2,1)} %param.8), channel_id=1, replica_groups=mesh['pb'=4,'ka'=4,'ga'=2] {'pb'}, dimensions={0}, use_global_device_ids=true | all-gather | bytes 245760 | tf_op jit(solution)/shard_map/all_gather | solution.py:111
  21.4 2.1 %fusion.3 = (f32[16,128]{1,0:T(8,128)S(1)}, f32[16,128]{1,0:T(8,128)S(1)}) fusion(bf16[16,128,256]{2,1,0:T(8,128)(2,1)} %param.10, bf16[16,128,256]{2,1,0:T(8,128)(2,1)} %param.11), kind=kLoop, calls=%fused_computation.16 | loop fusion | flops 2093056 | bytes 2113536 | tf_op jit(solution)/shard_map/hqd,hqd->hq/dot_general | solution.py:100
  23.6 0.6 exponential_multiply_fusion.1
  24.2 0.5 copy-done
  24.8 0.3 convolution_bitcast_fusion.3
  25.1 0.5 multiply_convert_fusion.1
  25.6 0.5 fusion.1
  26.1 0.8 exponential_multiply_fusion
  26.9 0.3 convolution_bitcast_fusion.2
  27.2 0.5 multiply_convert_fusion
  27.7 0.9 copy-done.2
  28.6 0.8 fusion
  29.5 1.1 copy.39
  30.6 0.5 convolution_multiply_fusion.1
  31.2 0.6 convolution_multiply_fusion
  31.7 1.9 %pad_maximum_fusion = f32[16,128,384]{1,2,0:T(8,128)} fusion(f32[16,128,192]{1,2,0:T(8,128)S(1)} %convolution_multiply_fusion, f32[16,128,192]{1,2,0:T(8,128)S(1)} %convolution_multiply_fusion.1), kind=kLoop, calls=%fused_computation | loop fusion | flops 786432 | bytes 6291456 | tf_op jit(solution)/shard_map/concatenate | solution.py:61
  33.7 21.0 %reduce-scatter.7.cloned.1.call-done = f32[64,640]{1,0:T(8,128)} async-done(((f32[256,640]{1,0:T(8,128)}), f32[64,640]{1,0:T(8,128)}) %reduce-scatter.7.cloned.1.call-update) | async-done | bytes 163856
  54.6 1.5 %slice.73 = f32[64,256]{1,0:T(8,128)} slice(f32[64,640]{1,0:T(8,128)} %reduce-scatter.7.cloned.1.call-done), slice={[0:64], [384:640]} | slice | bytes 131072 | tf_op jit(solution)/shard_map/slice | solution.py:119
  56.1 1.5 %slice.72 = f32[64,384]{1,0:T(8,128)} slice(f32[64,640]{1,0:T(8,128)} %reduce-scatter.7.cloned.1.call-done), slice={[0:64], [0:384]} | slice | bytes 196608 | tf_op jit(solution)/shard_map/slice | solution.py:118
  57.7 59.7 %reduce-scatter.5.cloned.1.call-done = f32[4,128,384]{1,2,0:T(8,128)} async-done(((f32[16,128,384]{1,2,0:T(8,128)}), f32[4,128,384]{1,2,0:T(8,128)}) %reduce-scatter.5.cloned.1.call-update) | async-done | bytes 786448 | tf_op jit(solution)/shard_map/reduce_scatter | solution.py:122
  117.4 2.3 %copy.24 = f32[4,128,384]{2,1,0:T(8,128)} copy(f32[4,128,384]{1,2,0:T(8,128)} %reduce-scatter.5.cloned.1.call-done) | data formatting | bytes 1572864
  (10 shorter events, 0.2 us)
Async XLA Ops:
  7.2 16.4 %copy-start.1 = (bf16[16,128,384]{2,1,0:T(8,128)(2,1)S(1)}, bf16[16,128,384]{2,1,0:T(8,128)(2,1)}, u32[]{:S(2)}) copy-start(bf16[16,128,384]{2,1,0:T(8,128)(2,1)} %param.7) | copy-start | bytes 4718596
  7.2 47.5 %reduce-scatter.7.cloned.1.call-start = ((), (), s32[]{:S(2)}) async-start(), calls=%async_computation.3 | async-start | bytes 819200
  23.5 1.2 copy-start
  27.2 1.4 %copy-start.2 = (bf16[16,128,384]{2,1,0:T(8,128)(2,1)S(1)}, bf16[16,128,384]{2,1,0:T(8,128)(2,1)}, u32[]{:S(2)}) copy-start(bf16[16,128,384]{2,1,0:T(8,128)(2,1)} %param.7) | copy-start | bytes 4718596
  30.6 86.8 %reduce-scatter.5.cloned.1.call-start = ((), (), s32[]{:S(2)}) async-start(), calls=%async_computation.2 | async-start | bytes 3932160 | tf_op jit(solution)/shard_map/reduce_scatter | solution.py:122
Sparse Core Ops, SparseCore 0:
  30.7 23.8 reduce-scatter.6
  56.9 60.3 reduce-scatter.4
where the time goes:
time: 127 us; the launch traced here: 126 us
  waiting for transfers between devices  80.7 us (64%)
  between operations  14.2 us (11%)
  blocking collectives  12.7 us (10%)
  local copies, waits for them, and re-layouts  8.57 us (7%)
  matrix products  5.4 us (4%)
  other arithmetic  4.88 us (4%)
    reduce_scatter x1, waiting for transfers between devices, per_device(): lax.psum_scatter(query_grad, 'ka', scatter_dimension=0, tiled=True)  59.7 us
    unnamed x3, waiting for transfers between devices  21 us
    all_gather x1, blocking collectives, per_device(): lax.all_gather(comp_values, 'pb', axis=0, tiled=True)  6.71 us
    all_gather x1, blocking collectives, per_device(): lax.all_gather(comp_keys, 'pb', axis=0, tiled=True)  5.97 us
    unnamed x8, local copies, waits for them, and re-layouts  4.84 us
  transfers between devices with their start and end apart: 2, of which 2 were waited for; matrix products, arithmetic and copies ran while one was open for 5% of the time, Pallas kernels for 0%

commit v1 on v0

v1 whole, which is shorter than its diff:
```python
import functools

import jax
import jax.numpy as jnp
from jax import lax
from jax.experimental import pallas as pl
from jax.experimental.pallas import tpu as pltpu
from jax.sharding import PartitionSpec as P

DK = 192
DV = 128
LANES = 128
MESH = pl.DeviceIdType.MESH


def flip(index, bits):
    bit = 1
    while bit <= bits:
        if bits & bit:
            index = index + bit - 2 * bit * ((index // bit) % 2)
        bit *= 2
    return index


def low_bit(m):
    return m & -m


def window(group):
    start = group * DK // LANES * LANES
    stop = -(-(group + 1) * DK // LANES) * LANES
    return start, stop


def keep_group(block, group):
    start, stop = window(group)
    lane = lax.broadcasted_iota(jnp.int32, block.shape, 1) + start
    inside = (lane >= group * DK) & (lane < (group + 1) * DK)
    return jnp.where(inside, block, jnp.zeros_like(block))


def dot(a, b, ca, cb):
    return lax.dot_general(a, b, (((ca,), (cb,)), ((), ())), preferred_element_type=jnp.float32)


def kernel(n_pb, n_ka, groups, heads, nq, rows, n_blocks, *refs):
    bits = n_pb.bit_length() - 1
    q_hbm, k_hbm, v_hbm, o_hbm, do_hbm, lse_hbm, vis_hbm = refs[:7]
    dq_ref, dk_ref, dv_ref = refs[7:10]
    (kv, qv, dov, ov, lse, vis, qm, stat, dq_acc, acc) = refs[10:20]
    rest = list(refs[20:])
    recvs = [rest.pop(0) for _ in range(bits)]
    sends = [None] + [rest.pop(0) for _ in range(bits - 1)]
    zs, zr, loc_sem, ag_s, ag_r, vs_s, vs_r, rs_s, rs_r, z_s, z_r = rest

    ka = lax.axis_index("ka")
    pb = lax.axis_index("pb")
    scale = DK ** (-0.5)
    dk_cols = groups * DK
    keys_ka = n_pb * rows
    hq = heads * nq

    locals_ = [
        (k_hbm, kv.at[ka, pb, :, pl.ds(0, dk_cols)]),
        (v_hbm, kv.at[ka, pb, :, pl.ds(dk_cols, groups * DV)]),
        (vis_hbm, vis.at[ka]),
        (q_hbm.at[pl.ds(ka * heads, heads)], qv),
        (do_hbm.at[pl.ds(ka * heads, heads)], dov),
        (o_hbm.at[pl.ds(ka * heads, heads)], ov),
        (lse_hbm, lse),
    ]
    loc = [pltpu.make_async_copy(a, b, loc_sem.at[i]) for i, (a, b) in enumerate(locals_)]
    for c in loc:
        c.start()

    barrier = pltpu.get_barrier_semaphore()
    for j in range(1, n_ka):
        pl.semaphore_signal(barrier, inc=1, device_id={"ka": flip(ka, j)}, device_id_type=MESH)
    for t in range(bits):
        pl.semaphore_signal(barrier, inc=1, device_id={"pb": flip(pb, 1 << t)}, device_id_type=MESH)
    for c in loc[:3]:
        c.wait()
    pl.semaphore_wait(barrier, n_ka - 1 + bits)

    pending = []

    def remote(src, dst, s_sem, r_sem, **peer):
        return pltpu.make_async_remote_copy(
            src_ref=src, dst_ref=dst, send_sem=s_sem, recv_sem=r_sem,
            device_id=peer, device_id_type=MESH,
        )

    def send(*args, **peer):
        copy = remote(*args, **peer)
        copy.start()
        pending.append(copy)

    def shard(j, m):
        return kv.at[flip(ka, j), flip(pb, m)]

    def wait_shard(j, m):
        peer = {"pb": flip(pb, low_bit(m))} if m else {"ka": flip(ka, j)}
        remote(shard(j, m), shard(j, m), ag_s.at[j, m], ag_r.at[j, m], **peer).wait_recv()

    def forward(j, m):
        bit = n_pb // 2
        while bit:
            if m == 0 or bit < low_bit(m):
                send(shard(j, m), shard(j, m), ag_s.at[j, m ^ bit], ag_r.at[j, m ^ bit], pb=flip(pb, bit))
            bit //= 2

    def relay(j):
        if j:
            wait_shard(j, 0)
            forward(j, 0)
        bit = n_pb // 2
        while bit > 1:
            for m in range(bit, n_pb, 2 * bit):
                wait_shard(j, m)
                forward(j, m)
            bit //= 2

    for j in range(1, n_ka):
        send(kv.at[ka, pb], kv.at[ka, pb], ag_s.at[j, 0], ag_r.at[j, 0], ka=flip(ka, j))
    forward(0, 0)
    for j in range(1, n_ka):
        send(vis.at[ka], vis.at[ka], vs_s.at[j], vs_r.at[j], ka=flip(ka, j))

    for c in loc[3:]:
        c.wait()
    for g in range(groups):
        start, stop = window(g)
        qm[g] = keep_group(qv[:, :, start:stop].reshape(hq, stop - start), g)
        product = dov[:, :, g * DV : (g + 1) * DV].astype(jnp.float32) * ov[
            :, :, g * DV : (g + 1) * DV
        ].astype(jnp.float32)
        row_delta = jnp.sum(jnp.transpose(product.reshape(hq, DV)), axis=0, keepdims=True)
        stat[2 * g + 1 : 2 * g + 2, :] = row_delta
        for h in range(heads):
            stat[2 * g : 2 * g + 1, h * nq : (h + 1) * nq] = lse[g, pl.ds(ka * heads + h, 1), :]

    per = min(n_pb, max(1, 256 // rows))
    chunk_rows = per * rows

    def compute_chunk(j, chunk):
        s = flip(ka, j)
        whole = kv[s, pl.ds(chunk * per, per)].reshape(chunk_rows, dk_cols + groups * DV)
        if per == n_pb:
            seen = vis[s]
        else:
            seen = vis[s, :, pl.ds(pl.multiple_of(chunk * chunk_rows, chunk_rows), chunk_rows)]
        seen = seen.astype(jnp.float32)
        block = lax.broadcasted_iota(jnp.int32, (nq, chunk_rows), 0) // (nq // n_blocks)
        mask = jnp.zeros((nq, chunk_rows), jnp.float32)
        for b in range(n_blocks):
            mask = jnp.where(block == b, seen[b : b + 1, :], mask)
        mask = jnp.transpose(mask)
        mask = jnp.concatenate([mask] * heads, axis=1)
        tiles = {}
        for g in range(groups):
            start, stop = window(g)
            keys = keep_group(whole[:, start:stop], g)
            values = whole[:, dk_cols + g * DV : dk_cols + (g + 1) * DV]
            grad = dov[:, :, g * DV : (g + 1) * DV].reshape(hq, DV)
            query = qm[g]
            scores = dot(keys, query, 1, 1) * scale
            probs = jnp.exp(scores - stat[2 * g : 2 * g + 1, :]) * mask
            grad_probs = dot(values, grad, 1, 1)
            grad_scores = (probs * (grad_probs - stat[2 * g + 1 : 2 * g + 2, :])).astype(jnp.bfloat16)
            value_grad = dot(probs.astype(jnp.bfloat16), grad, 1, 0)
            acc[j, pl.ds(chunk * per, per), :, dk_cols + g * DV : dk_cols + (g + 1) * DV] = (
                value_grad.reshape(per, rows, DV)
            )
            key_grad = dot(grad_scores, query, 1, 0)
            for c in range(start, stop, LANES):
                part = key_grad[:, c - start : c - start + LANES]
                tiles[c] = tiles[c] + part if c in tiles else part
            query_grad = dot(grad_scores, keys, 0, 0)
            dq_acc[:, start:stop] += query_grad
        for c, tile in tiles.items():
            acc[j, pl.ds(chunk * per, per), :, c : c + LANES] = tile.reshape(per, rows, LANES)

    def compute(j):
        for m in range(1, n_pb, 2):
            wait_shard(j, m)
        if j:
            s = flip(ka, j)
            remote(vis.at[s], vis.at[s], vs_s.at[j], vs_r.at[j], ka=s).wait_recv()
        if per == n_pb:
            compute_chunk(j, 0)
        else:
            lax.fori_loop(0, n_pb // per, lambda c, _: (compute_chunk(j, c), 0)[1], 0)
        for m in range(1, n_pb, 2):
            send(acc.at[j, flip(pb, m)], recvs[0].at[j, m >> 1], rs_s.at[j, m], rs_r.at[j, m], pb=flip(pb, 1))

    def reduce_stage(j, t):
        step = 2 << t
        for m in range(0, n_pb, step):
            slot = recvs[t].at[j, m >> (t + 1)]
            sem = m + (1 << t)
            remote(slot, slot, rs_s.at[j, sem], rs_r.at[j, sem], pb=flip(pb, 1 << t)).wait_recv()
            mine = flip(pb, m)
            total = acc[j, mine] + slot[...].astype(jnp.float32)
            if m & step:
                at = m >> (t + 2)
                sends[t + 1][j, at] = total.astype(jnp.bfloat16)
                send(
                    sends[t + 1].at[j, at], recvs[t + 1].at[j, at],
                    rs_s.at[j, m], rs_r.at[j, m], pb=flip(pb, step),
                )
            elif t == bits - 1 and j:
                zs[j] = total.astype(jnp.bfloat16)
                send(zs.at[j], zr.at[j], z_s.at[j], z_r.at[j], ka=flip(ka, j))
            else:
                acc[j, mine] = total

    dq_acc[...] = jnp.zeros_like(dq_acc)
    relay(0)
    relay(min(1, n_ka - 1))
    for i in range(n_ka + bits):
        if i < n_ka:
            compute(i)
        if i + 2 < n_ka:
            relay(i + 2)
        for t in range(bits - 1, -1, -1):
            if 0 <= i - 1 - t < n_ka:
                reduce_stage(i - 1 - t, t)
        if i == n_ka - 1:
            for h in range(heads):
                dq_ref[h] = dq_acc[h * nq : (h + 1) * nq, :] * scale

    total = acc[0, pb]
    for j in range(1, n_ka):
        remote(zr.at[j], zr.at[j], z_s.at[j], z_r.at[j], ka=flip(ka, j)).wait_recv()
        total = total + zr[j].astype(jnp.float32)
    dk_ref[...] = total[:, :dk_cols] * scale
    dv_ref[...] = total[:, dk_cols:]
    for copy in pending:
        copy.wait_send()


def per_device(n_pb, n_ka, queries, comp_keys, comp_values, outputs, grad_out, log_sums, visible):
    groups = comp_keys.shape[1] // DK
    all_heads, nq, _ = queries.shape
    heads = all_heads // n_ka
    rows = comp_keys.shape[0]
    cols = comp_keys.shape[1] + comp_values.shape[1]
    bits = n_pb.bit_length() - 1
    n_blocks = visible.shape[0]
    f32, bf16 = jnp.float32, jnp.bfloat16
    width = window(0)[1] - window(0)[0]
    hq = heads * nq
    scratch = [
        pltpu.VMEM((n_ka, n_pb, rows, cols), bf16),
        pltpu.VMEM((heads, nq, queries.shape[2]), bf16),
        pltpu.VMEM((heads, nq, grad_out.shape[2]), bf16),
        pltpu.VMEM((heads, nq, grad_out.shape[2]), bf16),
        pltpu.VMEM(log_sums.shape, f32),
        pltpu.VMEM((n_ka,) + visible.shape, jnp.int32),
        pltpu.VMEM((groups, hq, width), bf16),
        pltpu.VMEM((2 * groups, hq), f32),
        pltpu.VMEM((hq, groups * DK), f32),
        pltpu.VMEM((n_ka, n_pb, rows, cols), f32),
    ]
    scratch += [
        pltpu.VMEM((n_ka, n_pb >> (t + 1), rows, cols), f32 if t == 0 else bf16) for t in range(bits)
    ]
    scratch += [pltpu.VMEM((n_ka, n_pb >> (t + 1), rows, cols), bf16) for t in range(1, bits)]
    dma = pltpu.SemaphoreType.DMA
    scratch += [
        pltpu.VMEM((n_ka, rows, cols), bf16),
        pltpu.VMEM((n_ka, rows, cols), bf16),
        dma((7,)),
        dma((n_ka, n_pb)),
        dma((n_ka, n_pb)),
        dma((n_ka,)),
        dma((n_ka,)),
        dma((n_ka, n_pb)),
        dma((n_ka, n_pb)),
        dma((n_ka,)),
        dma((n_ka,)),
    ]
    return pl.pallas_call(
        functools.partial(kernel, n_pb, n_ka, groups, heads, nq, rows, n_blocks),
        out_shape=(
            jax.ShapeDtypeStruct((heads, nq, queries.shape[2]), f32),
            jax.ShapeDtypeStruct(comp_keys.shape, f32),
            jax.ShapeDtypeStruct(comp_values.shape, f32),
        ),
        in_specs=[pl.BlockSpec(memory_space=pl.ANY)] * 7,
        out_specs=[pl.BlockSpec(memory_space=pltpu.VMEM)] * 3,
        scratch_shapes=scratch,
        compiler_params=pltpu.CompilerParams(
            collective_id=0, has_side_effects=True, vmem_limit_bytes=64000 * 1024
        ),
    )(queries, comp_keys, comp_values, outputs, grad_out, log_sums, visible)


def solution(mesh):
    n_pb, n_ka = mesh.shape["pb"], mesh.shape["ka"]
    return jax.shard_map(
        functools.partial(per_device, n_pb, n_ka),
        mesh=mesh,
        in_specs=(
            P(None, "pb", "ga"),
            P(("ka", "pb"), "ga"),
            P(("ka", "pb"), "ga"),
            P(None, "pb", "ga"),
            P(None, "pb", "ga"),
            P("ga", None, "pb"),
            P("pb", "ka"),
        ),
        out_specs=(P("ka", "pb", "ga"), P(("ka", "pb"), "ga"), P(("ka", "pb"), "ga")),
        check_vma=False,
    )
```

time: 127 us -> 46.1 us (0.36)
  waiting for transfers between devices: 80.7 us -> 0 us
  Pallas kernels: 0 us -> 41.9 us
  between operations: 14.2 us -> 0.66 us
  blocking collectives: 12.7 us -> 0 us
  matrix products: 5.4 us -> 0 us
  local copies, waits for them, and re-layouts: 8.57 us -> 3.38 us
  other arithmetic: 4.88 us -> 0 us
    reduce_scatter x1 -> x0, waiting for transfers between devices: 59.7 us -> none  [per_device(): lax.psum_scatter(query_grad, 'ka', scatter_dimension=0, tiled=True)]
    pallas_call x0 -> x1, Pallas kernels: none -> 41.9 us  [per_device(): pl.pallas_call(functools.partial(kernel, n_pb, n_ka, groups, heads, nq, r...]
    unnamed x3 -> x0, waiting for transfers between devices: 21 us -> none
    all_gather x2 -> x0, blocking collectives: 12.7 us -> none  [the longest x1 6.71 us: per_device(): lax.all_gather(comp_values, 'pb', axis=0, tiled=True)]
    dot_general x10 -> x0, matrix products: 5.4 us -> none  [the longest x2 1.46 us: group_grads(): jnp.einsum('hqd,kd->hqk', query_group, key_group, preferred_element_type=...]
    slice x2 -> x0, local copies, waits for them, and re-layouts: 3.01 us -> none  [the longest x1 1.54 us: per_device(): key_out = stacked[:, :groups * DK]]
    dot_general x1 -> x0, other arithmetic: 2.13 us -> none  [per_device(): jnp.einsum('hqd,hqd->hq', grad_out[:, :, group_index * DV:(group_index +...]
    concatenate x2 -> x0, other arithmetic: 1.96 us -> none  [the longest x1 1.91 us: piece_grads(): jnp.concatenate([entry[0] for entry in results], axis=2)]
  transfers between devices with their start and end apart: 2 -> 0, of which waited for: 2 -> 0; matrix products, arithmetic and copies ran while one was open for 5% -> 0% of each run, Pallas kernels for 0% -> 0%
where the time goes in v1:
time: 46.1 us; the launch traced here: 45.9 us
  Pallas kernels  41.9 us (91%)
  local copies, waits for them, and re-layouts  3.38 us (7%)
  between operations  0.66 us (1%)
    pallas_call x1, Pallas kernels, per_device(): pl.pallas_call(functools.partial(kernel, n_pb, n_ka, groups, heads, nq, r...  41.9 us
    unnamed x7, local copies, waits for them, and re-layouts  3.38 us

profile of v1, /device:TPU:0, one launch (start us, length us, event | category | flops | bytes accessed | tf_op | source)
XLA Modules:
  0.0 45.9 jit_solution(15691225385923268096)
XLA Ops:
  0.6 41.9 %shard_map.94 = (f32[4,128,384]{2,1,0:T(8,128)}, f32[64,384]{1,0:T(8,128)}, f32[64,256]{1,0:T(8,128)}) custom-call(bf16[16,128,384]{2,1,0:T(8,128)(2,1)} %refs_0_.1, bf16[64,384]{1,0:T(8,128)(2,1)} %refs_1_.1, bf16[64,256]{1,0:T(8,128)(2,1)} %refs_2_.1, bf16[16,128,256]{2,1,0:T(8,128)(2,1)} %refs_3_.1, bf16[16,128,256]{2,1,0:T(8,128)(2,1)} %refs_4_.1, ...), custom_call_target="tpu_custom_call" | custom-call | tf_op jit(solution)/shard_map/pallas_call | solution.py:283
  42.5 0.0 copy-start
  42.5 0.0 copy-start.1
  42.5 2.1 %copy.13 = f32[4,128,384]{2,1,0:T(8,128)} copy(f32[4,128,384]{2,1,0:T(8,128)} %get-tuple-element.6) | data formatting | bytes 1572864
  44.6 0.0 copy-done
  44.6 0.6 %copy.14 = f32[64,384]{1,0:T(8,128)} copy(f32[64,384]{1,0:T(8,128)S(1)} %copy-done) | data formatting | bytes 196608
  45.3 0.0 copy-done.1
  45.3 0.6 %copy.15 = f32[64,256]{1,0:T(8,128)} copy(f32[64,256]{1,0:T(8,128)S(1)} %copy-done.1) | data formatting | bytes 131072
Async XLA Ops:
  42.5 2.1 %copy-start = (f32[64,384]{1,0:T(8,128)S(1)}, f32[64,384]{1,0:T(8,128)}, u32[]{:S(2)}) copy-start(f32[64,384]{1,0:T(8,128)} %get-tuple-element.7) | copy-start | bytes 294916
  42.5 2.8 %copy-start.1 = (f32[64,256]{1,0:T(8,128)S(1)}, f32[64,256]{1,0:T(8,128)}, u32[]{:S(2)}) copy-start(f32[64,256]{1,0:T(8,128)} %get-tuple-element.8) | copy-start | bytes 196612

commit v2 on v1

--- a/solution.py
+++ b/solution.py
@@ -26,47 +26,81 @@
     return m & -m
 
 
-def window(group):
-    start = group * DK // LANES * LANES
-    stop = -(-(group + 1) * DK // LANES) * LANES
-    return start, stop
+def tile_start(group):
+    return group * DK // LANES * LANES
 
 
 def keep_group(block, group):
-    start, stop = window(group)
-    lane = lax.broadcasted_iota(jnp.int32, block.shape, 1) + start
+    axis = block.ndim - 1
+    lane = lax.broadcasted_iota(jnp.int32, block.shape, axis) + tile_start(group)
     inside = (lane >= group * DK) & (lane < (group + 1) * DK)
     return jnp.where(inside, block, jnp.zeros_like(block))
 
 
+def half_roll(block):
+    return pltpu.roll(block, LANES // 2, block.ndim - 1)
+
+
+def pack(block, group):
+    first, second = block[..., :LANES], block[..., LANES:]
+    even = group % 2 == 0
+    full = jnp.where(even, first, second)
+    half = jnp.where(even, second, first)
+    rows = block.shape[1] // 2
+    return full, half[:, :rows] + half_roll(half[:, rows:])
+
+
+def unpack(full, folded, group):
+    even = group % 2 == 0
+    lane = lax.broadcasted_iota(jnp.int32, folded.shape, 2)
+    inside = (lane < LANES // 2) == even
+    low = jnp.where(inside, folded, 0.0)
+    high = jnp.where(inside, half_roll(folded), 0.0)
+    half = jnp.concatenate([low, high], axis=1)
+    return jnp.where(even, full, half), jnp.where(even, half, full)
+
+
 def dot(a, b, ca, cb):
     return lax.dot_general(a, b, (((ca,), (cb,)), ((), ())), preferred_element_type=jnp.float32)
 
 
-def kernel(n_pb, n_ka, groups, heads, nq, rows, n_blocks, *refs):
+def kernel(n_pb, n_ka, groups, own_heads, nq, rows, n_blocks, *refs):
     bits = n_pb.bit_length() - 1
     q_hbm, k_hbm, v_hbm, o_hbm, do_hbm, lse_hbm, vis_hbm = refs[:7]
     dq_ref, dk_ref, dv_ref = refs[7:10]
-    (kv, qv, dov, ov, lse, vis, qm, stat, dq_acc, acc) = refs[10:20]
-    rest = list(refs[20:])
+    (kv, own, qv, dov, ov, lse, vis, stat, dq_acc, dq_full, dq_s, dq_r, acc, whole_grad) = refs[10:24]
+    rest = list(refs[24:])
     recvs = [rest.pop(0) for _ in range(bits)]
     sends = [None] + [rest.pop(0) for _ in range(bits - 1)]
-    zs, zr, loc_sem, ag_s, ag_r, vs_s, vs_r, rs_s, rs_r, z_s, z_r = rest
+    zs, zr, loc_sem, ag_s, ag_r, vs_s, vs_r, rs_s, rs_r, z_s, z_r, q_s, q_r = rest
 
     ka = lax.axis_index("ka")
     pb = lax.axis_index("pb")
     scale = DK ** (-0.5)
-    dk_cols = groups * DK
-    keys_ka = n_pb * rows
+    width = 2 * LANES
+    heads = own_heads * groups
+    group = ka % groups
+    first_head = (ka // groups) * heads
     hq = heads * nq
+    k_start = pl.multiple_of(tile_start(group), LANES)
+    v_start = pl.multiple_of(group * DV, LANES)
+    head_part = pl.ds(first_head, heads)
 
     locals_ = [
-        (k_hbm, kv.at[ka, pb, :, pl.ds(0, dk_cols)]),
-        (v_hbm, kv.at[ka, pb, :, pl.ds(dk_cols, groups * DV)]),
-        (vis_hbm, vis.at[ka]),
-        (q_hbm.at[pl.ds(ka * heads, heads)], qv),
-        (do_hbm.at[pl.ds(ka * heads, heads)], dov),
-        (o_hbm.at[pl.ds(ka * heads, heads)], ov),
+        (k_hbm.at[:, pl.ds(k_start, width)], kv.at[ka, pb, :, pl.ds(0, width)]),
+        (v_hbm.at[:, pl.ds(v_start, DV)], kv.at[ka, pb, :, pl.ds(width, DV)]),
+    ]
+    for g in range(groups):
+        locals_ += [
+            (k_hbm.at[:, pl.ds(tile_start(g), width)], own.at[g, :, pl.ds(0, width)]),
+            (v_hbm.at[:, pl.ds(g * DV, DV)], own.at[g, :, pl.ds(width, DV)]),
+        ]
+    locals_ += [(vis_hbm, vis.at[ka])]
+    first = len(locals_)
+    locals_ += [
+        (q_hbm.at[head_part, :, pl.ds(k_start, width)], qv),
+        (do_hbm.at[head_part, :, pl.ds(v_start, DV)], dov),
+        (o_hbm.at[head_part, :, pl.ds(v_start, DV)], ov),
         (lse_hbm, lse),
     ]
     loc = [pltpu.make_async_copy(a, b, loc_sem.at[i]) for i, (a, b) in enumerate(locals_)]
@@ -78,7 +112,7 @@
         pl.semaphore_signal(barrier, inc=1, device_id={"ka": flip(ka, j)}, device_id_type=MESH)
     for t in range(bits):
         pl.semaphore_signal(barrier, inc=1, device_id={"pb": flip(pb, 1 << t)}, device_id_type=MESH)
-    for c in loc[:3]:
+    for c in loc[:first]:
         c.wait()
     pl.semaphore_wait(barrier, n_ka - 1 + bits)
 
@@ -121,30 +155,27 @@
             bit //= 2
 
     for j in range(1, n_ka):
-        send(kv.at[ka, pb], kv.at[ka, pb], ag_s.at[j, 0], ag_r.at[j, 0], ka=flip(ka, j))
+        far = flip(ka, j)
+        send(own.at[far % groups], kv.at[ka, pb], ag_s.at[j, 0], ag_r.at[j, 0], ka=far)
     forward(0, 0)
     for j in range(1, n_ka):
         send(vis.at[ka], vis.at[ka], vs_s.at[j], vs_r.at[j], ka=flip(ka, j))
 
-    for c in loc[3:]:
+    for c in loc[first:]:
         c.wait()
-    for g in range(groups):
-        start, stop = window(g)
-        qm[g] = keep_group(qv[:, :, start:stop].reshape(hq, stop - start), g)
-        product = dov[:, :, g * DV : (g + 1) * DV].astype(jnp.float32) * ov[
-            :, :, g * DV : (g + 1) * DV
-        ].astype(jnp.float32)
-        row_delta = jnp.sum(jnp.transpose(product.reshape(hq, DV)), axis=0, keepdims=True)
-        stat[2 * g + 1 : 2 * g + 2, :] = row_delta
-        for h in range(heads):
-            stat[2 * g : 2 * g + 1, h * nq : (h + 1) * nq] = lse[g, pl.ds(ka * heads + h, 1), :]
+    qv[...] = keep_group(qv[...], group)
+    product = dov[...].astype(jnp.float32) * ov[...].astype(jnp.float32)
+    stat[1:2, :] = jnp.sum(jnp.transpose(product.reshape(hq, DV)), axis=0, keepdims=True)
+    for h in range(heads):
+        stat[0:1, h * nq : (h + 1) * nq] = lse[group, pl.ds(first_head + h, 1), :]
+    dq_acc[...] = jnp.zeros_like(dq_acc)
 
     per = min(n_pb, max(1, 256 // rows))
     chunk_rows = per * rows
 
     def compute_chunk(j, chunk):
         s = flip(ka, j)
-        whole = kv[s, pl.ds(chunk * per, per)].reshape(chunk_rows, dk_cols + groups * DV)
+        whole = kv[s, pl.ds(chunk * per, per)].reshape(chunk_rows, width + DV)
         if per == n_pb:
             seen = vis[s]
         else:
@@ -156,29 +187,22 @@
             mask = jnp.where(block == b, seen[b : b + 1, :], mask)
         mask = jnp.transpose(mask)
         mask = jnp.concatenate([mask] * heads, axis=1)
-        tiles = {}
-        for g in range(groups):
-            start, stop = window(g)
-            keys = keep_group(whole[:, start:stop], g)
-            values = whole[:, dk_cols + g * DV : dk_cols + (g + 1) * DV]
-            grad = dov[:, :, g * DV : (g + 1) * DV].reshape(hq, DV)
-            query = qm[g]
-            scores = dot(keys, query, 1, 1) * scale
-            probs = jnp.exp(scores - stat[2 * g : 2 * g + 1, :]) * mask
-            grad_probs = dot(values, grad, 1, 1)
-            grad_scores = (probs * (grad_probs - stat[2 * g + 1 : 2 * g + 2, :])).astype(jnp.bfloat16)
-            value_grad = dot(probs.astype(jnp.bfloat16), grad, 1, 0)
-            acc[j, pl.ds(chunk * per, per), :, dk_cols + g * DV : dk_cols + (g + 1) * DV] = (
-                value_grad.reshape(per, rows, DV)
-            )
-            key_grad = dot(grad_scores, query, 1, 0)
-            for c in range(start, stop, LANES):
-                part = key_grad[:, c - start : c - start + LANES]
-                tiles[c] = tiles[c] + part if c in tiles else part
-            query_grad = dot(grad_scores, keys, 0, 0)
-            dq_acc[:, start:stop] += query_grad
-        for c, tile in tiles.items():
-            acc[j, pl.ds(chunk * per, per), :, c : c + LANES] = tile.reshape(per, rows, LANES)
+        keys = keep_group(whole[:, :width], group)
+        values = whole[:, width:]
+        grad = dov[...].reshape(hq, DV)
+        query = qv[...].reshape(hq, width)
+        scores = dot(keys, query, 1, 1) * scale
+        probs = jnp.exp(scores - stat[0:1, :]) * mask
+        grad_probs = dot(values, grad, 1, 1)
+        grad_scores = (probs * (grad_probs - stat[1:2, :])).astype(jnp.bfloat16)
+        value_grad = dot(probs.astype(jnp.bfloat16), grad, 1, 0)
+        at = pl.ds(chunk * per, per)
+        acc[j, at, 0:rows] = value_grad.reshape(per, rows, DV)
+        key_grad = dot(grad_scores, query, 1, 0)
+        full, folded = pack(key_grad.reshape(per, rows, width), group)
+        acc[j, at, rows : 2 * rows] = full
+        acc[j, at, 2 * rows :] = folded
+        dq_acc[...] += dot(grad_scores, keys, 0, 0)
 
     def compute(j):
         for m in range(1, n_pb, 2):
@@ -214,7 +238,17 @@
             else:
                 acc[j, mine] = total
 
-    dq_acc[...] = jnp.zeros_like(dq_acc)
+    def send_queries():
+        for r in range(1, groups):
+            far = flip(ka, r)
+            part = dq_acc[pl.ds(pl.multiple_of((far % groups) * own_heads * nq, nq), own_heads * nq), :]
+            full, folded = pack(part.reshape(own_heads, nq, width), group)
+            dq_s[r, :, :nq] = full.astype(jnp.bfloat16)
+            dq_s[r, :, nq:] = folded.astype(jnp.bfloat16)
+            send(dq_s.at[r], dq_r.at[r], q_s.at[r], q_r.at[r], ka=far)
+        mine = dq_acc[pl.ds(pl.multiple_of(group * own_heads * nq, nq), own_heads * nq), :]
+        dq_full[group] = mine.reshape(own_heads, nq, width)
+
     relay(0)
     relay(min(1, n_ka - 1))
     for i in range(n_ka + bits):
@@ -222,19 +256,49 @@
             compute(i)
         if i + 2 < n_ka:
             relay(i + 2)
+        if i == n_ka - 1:
+            send_queries()
         for t in range(bits - 1, -1, -1):
             if 0 <= i - 1 - t < n_ka:
                 reduce_stage(i - 1 - t, t)
-        if i == n_ka - 1:
-            for h in range(heads):
-                dq_ref[h] = dq_acc[h * nq : (h + 1) * nq, :] * scale
-
-    total = acc[0, pb]
+
+    def join(pieces, columns):
+        tiles = {}
+        for g in range(groups):
+            for c in range(2):
+                at = tile_start(g) + c * LANES
+                tile = pieces[g][c]
+                tiles[at] = tiles[at] + tile if at in tiles else tile
+        return [(at, tile) for at, tile in tiles.items() if at < columns]
+
+    for r in range(1, groups):
+        far = flip(ka, r)
+        remote(dq_r.at[r], dq_r.at[r], q_s.at[r], q_r.at[r], ka=far).wait_recv()
+        got = dq_r[r].astype(jnp.float32)
+        left, right = unpack(got[:, :nq], got[:, nq:], far % groups)
+        dq_full[far % groups, :, :, :LANES] = left
+        dq_full[far % groups, :, :, LANES:] = right
+    pieces = [(dq_full[g, :, :, :LANES], dq_full[g, :, :, LANES:]) for g in range(groups)]
+    for at, tile in join(pieces, groups * DK):
+        dq_ref[:, :, at : at + LANES] = tile * scale
+
+    totals = [acc[0, pb]] + [None] * (groups - 1)
     for j in range(1, n_ka):
         remote(zr.at[j], zr.at[j], z_s.at[j], z_r.at[j], ka=flip(ka, j)).wait_recv()
-        total = total + zr[j].astype(jnp.float32)
-    dk_ref[...] = total[:, :dk_cols] * scale
-    dv_ref[...] = total[:, dk_cols:]
+        term = zr[j].astype(jnp.float32)
+        r = j % groups
+        totals[r] = term if totals[r] is None else totals[r] + term
+    for r in range(groups):
+        whole_grad[flip(group, r)] = totals[r]
+    pieces = []
+    for g in range(groups):
+        dv_ref[:, g * DV : (g + 1) * DV] = whole_grad[g, 0:rows]
+        left, right = unpack(
+            whole_grad[g, rows : 2 * rows][None], whole_grad[g, 2 * rows :][None], jnp.int32(g)
+        )
+        pieces.append((left[0], right[0]))
+    for at, tile in join(pieces, groups * DK):
+        dk_ref[:, at : at + LANES] = tile * scale
     for copy in pending:
         copy.wait_send()
 
@@ -244,33 +308,38 @@
     all_heads, nq, _ = queries.shape
     heads = all_heads // n_ka
     rows = comp_keys.shape[0]
-    cols = comp_keys.shape[1] + comp_values.shape[1]
     bits = n_pb.bit_length() - 1
     n_blocks = visible.shape[0]
     f32, bf16 = jnp.float32, jnp.bfloat16
-    width = window(0)[1] - window(0)[0]
-    hq = heads * nq
+    width = 2 * LANES
+    team = heads * groups
+    packed = 2 * rows + rows // 2
     scratch = [
-        pltpu.VMEM((n_ka, n_pb, rows, cols), bf16),
-        pltpu.VMEM((heads, nq, queries.shape[2]), bf16),
-        pltpu.VMEM((heads, nq, grad_out.shape[2]), bf16),
-        pltpu.VMEM((heads, nq, grad_out.shape[2]), bf16),
+        pltpu.VMEM((n_ka, n_pb, rows, width + DV), bf16),
+        pltpu.VMEM((groups, rows, width + DV), bf16),
+        pltpu.VMEM((team, nq, width), bf16),
+        pltpu.VMEM((team, nq, DV), bf16),
+        pltpu.VMEM((team, nq, DV), bf16),
         pltpu.VMEM(log_sums.shape, f32),
         pltpu.VMEM((n_ka,) + visible.shape, jnp.int32),
-        pltpu.VMEM((groups, hq, width), bf16),
-        pltpu.VMEM((2 * groups, hq), f32),
-        pltpu.VMEM((hq, groups * DK), f32),
-        pltpu.VMEM((n_ka, n_pb, rows, cols), f32),
+        pltpu.VMEM((2, team * nq), f32),
+        pltpu.VMEM((team * nq, width), f32),
+        pltpu.VMEM((groups, heads, nq, width), f32),
+        pltpu.VMEM((groups, heads, nq + nq // 2, LANES), bf16),
+        pltpu.VMEM((groups, heads, nq + nq // 2, LANES), bf16),
+        pltpu.VMEM((n_ka, n_pb, packed, LANES), f32),
+        pltpu.VMEM((groups, packed, LANES), f32),
     ]
     scratch += [
-        pltpu.VMEM((n_ka, n_pb >> (t + 1), rows, cols), f32 if t == 0 else bf16) for t in range(bits)
-    ]
-    scratch += [pltpu.VMEM((n_ka, n_pb >> (t + 1), rows, cols), bf16) for t in range(1, bits)]
+        pltpu.VMEM((n_ka, n_pb >> (t + 1), packed, LANES), f32 if t == 0 else bf16)
+        for t in range(bits)
+    ]
+    scratch += [pltpu.VMEM((n_ka, n_pb >> (t + 1), packed, LANES), bf16) for t in range(1, bits)]
     dma = pltpu.SemaphoreType.DMA
     scratch += [
-        pltpu.VMEM((n_ka, rows, cols), bf16),
-        pltpu.VMEM((n_ka, rows, cols), bf16),
-        dma((7,)),
+        pltpu.VMEM((n_ka, packed, LANES), bf16),
+        pltpu.VMEM((n_ka, packed, LANES), bf16),
+        dma((7 + 2 * groups,)),
         dma((n_ka, n_pb)),
         dma((n_ka, n_pb)),
         dma((n_ka,)),
@@ -279,6 +348,8 @@
         dma((n_ka, n_pb)),
         dma((n_ka,)),
         dma((n_ka,)),
+        dma((groups,)),
+        dma((groups,)),
     ]
     return pl.pallas_call(
         functools.partial(kernel, n_pb, n_ka, groups, heads, nq, rows, n_blocks),

time: 46.1 us -> 41.6 us (0.902)
  Pallas kernels: 41.9 us -> 37.4 us
    pallas_call x1, Pallas kernels: 41.9 us -> 37.4 us  [per_device(): pl.pallas_call(functools.partial(kernel, n_pb, n_ka, groups, heads, nq, r...]
where the time goes in v2:
time: 41.6 us; the launch traced here: 41.4 us
  Pallas kernels  37.4 us (90%)
  local copies, waits for them, and re-layouts  3.38 us (8%)
  between operations  0.66 us (2%)
    pallas_call x1, Pallas kernels, per_device(): pl.pallas_call(functools.partial(kernel, n_pb, n_ka, groups, heads, nq, r...  37.4 us
    unnamed x7, local copies, waits for them, and re-layouts  3.38 us

profile of v2, /device:TPU:0, one launch (start us, length us, event | category | flops | bytes accessed | tf_op | source)
XLA Modules:
  0.0 41.4 jit_solution(5033477448320093897)
XLA Ops:
  0.6 37.4 %shard_map.94 = (f32[4,128,384]{2,1,0:T(8,128)}, f32[64,384]{1,0:T(8,128)}, f32[64,256]{1,0:T(8,128)}) custom-call(bf16[16,128,384]{2,1,0:T(8,128)(2,1)} %refs_0_.1, bf16[64,384]{1,0:T(8,128)(2,1)} %refs_1_.1, bf16[64,256]{1,0:T(8,128)(2,1)} %refs_2_.1, bf16[16,128,256]{2,1,0:T(8,128)(2,1)} %refs_3_.1, bf16[16,128,256]{2,1,0:T(8,128)(2,1)} %refs_4_.1, ...), custom_call_target="tpu_custom_call" | custom-call | tf_op jit(solution)/shard_map/pallas_call | solution.py:354
  38.0 0.0 copy-start
  38.1 0.0 copy-start.1
  38.1 2.1 %copy.13 = f32[4,128,384]{2,1,0:T(8,128)} copy(f32[4,128,384]{2,1,0:T(8,128)} %get-tuple-element.6) | data formatting | bytes 1572864
  40.2 0.0 copy-done
  40.2 0.6 %copy.14 = f32[64,384]{1,0:T(8,128)} copy(f32[64,384]{1,0:T(8,128)S(1)} %copy-done) | data formatting | bytes 196608
  40.8 0.0 copy-done.1
  40.8 0.6 %copy.15 = f32[64,256]{1,0:T(8,128)} copy(f32[64,256]{1,0:T(8,128)S(1)} %copy-done.1) | data formatting | bytes 131072
Async XLA Ops:
  38.0 2.1 %copy-start = (f32[64,384]{1,0:T(8,128)S(1)}, f32[64,384]{1,0:T(8,128)}, u32[]{:S(2)}) copy-start(f32[64,384]{1,0:T(8,128)} %get-tuple-element.7) | copy-start | bytes 294916
  38.1 2.8 %copy-start.1 = (f32[64,256]{1,0:T(8,128)S(1)}, f32[64,256]{1,0:T(8,128)}, u32[]{:S(2)}) copy-start(f32[64,256]{1,0:T(8,128)} %get-tuple-element.8) | copy-start | bytes 196612

commit v3 on v2

--- a/solution.py
+++ b/solution.py
@@ -143,16 +143,23 @@
                 send(shard(j, m), shard(j, m), ag_s.at[j, m ^ bit], ag_r.at[j, m ^ bit], pb=flip(pb, bit))
             bit //= 2
 
-    def relay(j):
-        if j:
-            wait_shard(j, 0)
-            forward(j, 0)
-        bit = n_pb // 2
-        while bit > 1:
-            for m in range(bit, n_pb, 2 * bit):
-                wait_shard(j, m)
-                forward(j, m)
-            bit //= 2
+    reached = {"z": 1, "x": 0}
+
+    def relay_z(upto):
+        while reached["z"] < min(upto, n_ka):
+            wait_shard(reached["z"], 0)
+            forward(reached["z"], 0)
+            reached["z"] += 1
+
+    def relay_x(upto):
+        while reached["x"] < min(upto, n_ka):
+            bit = n_pb // 2
+            while bit > 1:
+                for m in range(bit, n_pb, 2 * bit):
+                    wait_shard(reached["x"], m)
+                    forward(reached["x"], m)
+                bit //= 2
+            reached["x"] += 1
 
     for j in range(1, n_ka):
         far = flip(ka, j)
@@ -249,13 +256,13 @@
         mine = dq_acc[pl.ds(pl.multiple_of(group * own_heads * nq, nq), own_heads * nq), :]
         dq_full[group] = mine.reshape(own_heads, nq, width)
 
-    relay(0)
-    relay(min(1, n_ka - 1))
+    relay_z(2)
+    relay_x(1)
     for i in range(n_ka + bits):
         if i < n_ka:
             compute(i)
-        if i + 2 < n_ka:
-            relay(i + 2)
+        relay_z(i + 4)
+        relay_x(i + 2 if i == 0 else i + 3)
         if i == n_ka - 1:
             send_queries()
         for t in range(bits - 1, -1, -1):
@@ -354,9 +361,9 @@
     return pl.pallas_call(
         functools.partial(kernel, n_pb, n_ka, groups, heads, nq, rows, n_blocks),
         out_shape=(
-            jax.ShapeDtypeStruct((heads, nq, queries.shape[2]), f32),
-            jax.ShapeDtypeStruct(comp_keys.shape, f32),
-            jax.ShapeDtypeStruct(comp_values.shape, f32),
+            pltpu.VMEM((heads, nq, queries.shape[2]), f32),
+            pltpu.VMEM(comp_keys.shape, f32),
+            pltpu.VMEM(comp_values.shape, f32),
         ),
         in_specs=[pl.BlockSpec(memory_space=pl.ANY)] * 7,
         out_specs=[pl.BlockSpec(memory_space=pltpu.VMEM)] * 3,

time: 41.6 us -> 34.6 us (0.83)
  Pallas kernels: 37.4 us -> 31.7 us
  local copies, waits for them, and re-layouts: 3.38 us -> 2.15 us
    pallas_call x1, Pallas kernels: 37.4 us -> 31.7 us  [per_device(): pl.pallas_call(functools.partial(kernel, n_pb, n_ka, groups, heads, nq, r...]
    unnamed x7 -> x3, local copies, waits for them, and re-layouts: 3.38 us -> 2.15 us
where the time goes in v3:
time: 34.6 us; the launch traced here: 34.5 us
  Pallas kernels  31.7 us (92%)
  local copies, waits for them, and re-layouts  2.15 us (6%)
  between operations  0.64 us (2%)
    pallas_call x1, Pallas kernels, per_device(): pl.pallas_call(functools.partial(kernel, n_pb, n_ka, groups, heads, nq, r...  31.7 us
    unnamed x3, local copies, waits for them, and re-layouts  2.15 us

profile of v3, /device:TPU:0, one launch (start us, length us, event | category | flops | bytes accessed | tf_op | source)
XLA Modules:
  0.0 34.5 jit_solution(7076958817889603139)
XLA Ops:
  0.6 31.7 %shard_map.94 = (f32[4,128,384]{2,1,0:T(8,128)S(1)}, f32[64,384]{1,0:T(8,128)S(1)}, f32[64,256]{1,0:T(8,128)S(1)}) custom-call(bf16[16,128,384]{2,1,0:T(8,128)(2,1)} %refs_0_.1, bf16[64,384]{1,0:T(8,128)(2,1)} %refs_1_.1, bf16[64,256]{1,0:T(8,128)(2,1)} %refs_2_.1, bf16[16,128,256]{2,1,0:T(8,128)(2,1)} %refs_3_.1, bf16[16,128,256]{2,1,0:T(8,128)(2,1)} %refs_4_.1, ...), custom_call_target="tpu_custom_call" | custom-call | tf_op jit(solution)/shard_map/pallas_call | solution.py:361
  32.3 0.9 %copy.13 = f32[4,128,384]{2,1,0:T(8,128)} copy(f32[4,128,384]{2,1,0:T(8,128)S(1)} %get-tuple-element.3) | data formatting | bytes 1572864
  33.2 0.6 %copy.15 = f32[64,256]{1,0:T(8,128)} copy(f32[64,256]{1,0:T(8,128)S(1)} %get-tuple-element.5) | data formatting | bytes 131072
  33.8 0.6 %copy.14 = f32[64,384]{1,0:T(8,128)} copy(f32[64,384]{1,0:T(8,128)S(1)} %get-tuple-element.4) | data formatting | bytes 196608

commit v4 on v3

--- a/solution.py
+++ b/solution.py
@@ -161,7 +161,7 @@
                 bit //= 2
             reached["x"] += 1
 
-    for j in range(1, n_ka):
+    for j in range(n_ka - 1, 0, -1):
         far = flip(ka, j)
         send(own.at[far % groups], kv.at[ka, pb], ag_s.at[j, 0], ag_r.at[j, 0], ka=far)
     forward(0, 0)
@@ -258,16 +258,25 @@
 
     relay_z(2)
     relay_x(1)
+    reduced = set()
+
+    def reduce_once(j, t):
+        if 0 <= j < n_ka and (j, t) not in reduced:
+            reduced.add((j, t))
+            reduce_stage(j, t)
+
     for i in range(n_ka + bits):
         if i < n_ka:
             compute(i)
         relay_z(i + 4)
+        if i == 1:
+            reduce_once(0, 0)
+            reduce_once(1, 0)
         relay_x(i + 2 if i == 0 else i + 3)
         if i == n_ka - 1:
             send_queries()
-        for t in range(bits - 1, -1, -1):
-            if 0 <= i - 1 - t < n_ka:
-                reduce_stage(i - 1 - t, t)
+        for t in range(bits):
+            reduce_once(i - 1 - t, t)
 
     def join(pieces, columns):
         tiles = {}

time: 34.6 us -> 32.3 us (0.934)
  Pallas kernels: 31.7 us -> 29.4 us
    pallas_call x1, Pallas kernels: 31.7 us -> 29.4 us  [per_device(): pl.pallas_call(functools.partial(kernel, n_pb, n_ka, groups, heads, nq, r...]
where the time goes in v4:
time: 32.3 us; the launch traced here: 32.2 us
  Pallas kernels  29.4 us (91%)
  local copies, waits for them, and re-layouts  2.15 us (7%)
  between operations  0.64 us (2%)
    pallas_call x1, Pallas kernels, per_device(): pl.pallas_call(functools.partial(kernel, n_pb, n_ka, groups, heads, nq, r...  29.4 us
    unnamed x3, local copies, waits for them, and re-layouts  2.15 us

profile of v4, /device:TPU:0, one launch (start us, length us, event | category | flops | bytes accessed | tf_op | source)
XLA Modules:
  0.0 32.2 jit_solution(13728874136061121705)
XLA Ops:
  0.6 29.4 %shard_map.94 = (f32[4,128,384]{2,1,0:T(8,128)S(1)}, f32[64,384]{1,0:T(8,128)S(1)}, f32[64,256]{1,0:T(8,128)S(1)}) custom-call(bf16[16,128,384]{2,1,0:T(8,128)(2,1)} %refs_0_.1, bf16[64,384]{1,0:T(8,128)(2,1)} %refs_1_.1, bf16[64,256]{1,0:T(8,128)(2,1)} %refs_2_.1, bf16[16,128,256]{2,1,0:T(8,128)(2,1)} %refs_3_.1, bf16[16,128,256]{2,1,0:T(8,128)(2,1)} %refs_4_.1, ...), custom_call_target="tpu_custom_call" | custom-call | tf_op jit(solution)/shard_map/pallas_call | solution.py:370
  30.0 0.9 %copy.13 = f32[4,128,384]{2,1,0:T(8,128)} copy(f32[4,128,384]{2,1,0:T(8,128)S(1)} %get-tuple-element.3) | data formatting | bytes 1572864
  30.9 0.6 %copy.15 = f32[64,256]{1,0:T(8,128)} copy(f32[64,256]{1,0:T(8,128)S(1)} %get-tuple-element.5) | data formatting | bytes 131072
  31.5 0.6 %copy.14 = f32[64,384]{1,0:T(8,128)} copy(f32[64,384]{1,0:T(8,128)S(1)} %get-tuple-element.4) | data formatting | bytes 196608
